TPU v7x, 32 devices: a whole 2x2x4 slice. The times are simulated.
32 devices in a mesh: row: 4 (over y, x), col: 8 (over z, core).
Axes of the slice: x: 2, y: 2, z: 4, core: 2. Of those that a mesh axis runs over, the one named last changes fastest.
Arguments:
- pixels: float32 [3, 192, 256], P(None, 'row', 'col'), may hold values from -6 to 6
- stem_weight: bfloat16 [64, 3, 4, 4], replicated, may hold values from -0.875 to 0.875
- first_weight: bfloat16 [64, 64, 3, 3], replicated, may hold values from -0.25 to 0.25
- second_weight: bfloat16 [64, 64, 3, 3], replicated, may hold values from -0.25 to 0.25
- entry_weight: bfloat16 [256, 64, 3, 3], P('col'), may hold values from -0.25 to 0.25
- final_weight: bfloat16 [256, 256, 3, 3], P('col'), may hold values from -0.125 to 0.125
- upstream: bfloat16 [256, 96, 128], P('col', 'row'), may hold values from -6 to 6
Outputs:
- stem_grad: float32 [64, 3, 4, 4], replicated
- first_grad: float32 [64, 64, 3, 3], replicated
- second_grad: float32 [64, 64, 3, 3], replicated
- entry_grad: float32 [256, 64, 3, 3], P('col')
- final_grad: float32 [256, 256, 3, 3], P('col')
All inputs are finite; a program needn't handle non-finite values.
Results may differ from a plain program's by a relative error of at most 0.023.
Values may be sent and summed in bfloat16 or wider, within the bound.
A program may use at most 64 MiB of HBM per device.

v0:
```python
import functools
import math

import jax
import jax.numpy as jnp
from jax import lax
from jax.experimental import pallas as pl
from jax.experimental.pallas import tpu as pltpu
from jax.sharding import PartitionSpec as P

BF = jnp.bfloat16
F32 = jnp.float32


MESH = pl.DeviceIdType.MESH
VMEM = pl.BlockSpec(memory_space=pltpu.VMEM)
RIM = 16
UP_RIM = 4


def start_kernel(rows_of, cols_of, pix_ref, up_ref, pix_out, up_out, sends, pix_recv, rim_recv, up_recv, own_sems):
    row, col = lax.axis_index("row"), lax.axis_index("col")
    tall, up_rows = pix_ref.shape[0], up_ref.shape[0]
    barrier = pltpu.get_barrier_semaphore()
    not_first, not_last = row > 0, row < rows_of - 1

    for k in range(1, cols_of):
        peer = lax.rem(col + k, cols_of)
        pl.semaphore_signal(barrier, inc=1, device_id=(row, peer), device_id_type=MESH)
    for side, there in ((-1, not_first), (1, not_last)):

        @pl.when(there)
        def _():
            for k in range(cols_of):
                peer = lax.rem(col + k, cols_of)
                pl.semaphore_signal(
                    barrier, inc=1, device_id=(row + side, peer), device_id_type=MESH
                )

    bands = 1 + not_first.astype(jnp.int32) + not_last.astype(jnp.int32)
    pl.semaphore_wait(barrier, bands * cols_of - 1)

    def tile_copy(k):
        return pltpu.make_async_remote_copy(
            src_ref=pix_ref,
            dst_ref=pix_out.at[k, RIM : RIM + tall],
            send_sem=sends.at[0, k],
            recv_sem=pix_recv.at[k],
            device_id=(row, lax.rem(col + k, cols_of)),
            device_id_type=MESH,
        )

    def rim_copy(side, k):
        src = pix_ref.at[0:RIM] if side < 0 else pix_ref.at[tall - RIM : tall]
        dst = pix_out.at[k, RIM + tall : tall + 2 * RIM] if side < 0 else pix_out.at[k, 0:RIM]
        at = 0 if side < 0 else 1
        return pltpu.make_async_remote_copy(
            src_ref=src,
            dst_ref=dst,
            send_sem=sends.at[1 + at, k],
            recv_sem=rim_recv.at[at, k],
            device_id=(row + side, lax.rem(col + k, cols_of)),
            device_id_type=MESH,
        )

    def up_copy(side):
        src = up_ref.at[0:UP_RIM] if side < 0 else up_ref.at[up_rows - UP_RIM : up_rows]
        dst = up_out.at[UP_RIM + up_rows : up_rows + 2 * UP_RIM] if side < 0 else up_out.at[0:UP_RIM]
        at = 0 if side < 0 else 1
        return pltpu.make_async_remote_copy(
            src_ref=src,
            dst_ref=dst,
            send_sem=sends.at[3, at],
            recv_sem=up_recv.at[at],
            device_id=(row + side, col),
            device_id_type=MESH,
        )

    sides = ((-1, not_first), (1, not_last))
    for side, there in sides:

        @pl.when(there)
        def _():
            up_copy(side).start()
            for k in range(cols_of):
                rim_copy(side, k).start()

    for k in range(1, cols_of):
        tile_copy(k).start()
    own_pix = pltpu.make_async_copy(pix_ref, pix_out.at[0, RIM : RIM + tall], own_sems.at[0])
    own_up = pltpu.make_async_copy(up_ref, up_out.at[UP_RIM : UP_RIM + up_rows], own_sems.at[1])
    own_pix.start()
    own_up.start()

    @pl.when(row == 0)
    def _():
        for k in range(cols_of):
            pix_out[k, 0:RIM] = jnp.zeros((RIM, pix_ref.shape[1]), BF)
        up_out[0:UP_RIM] = jnp.zeros((UP_RIM,) + up_ref.shape[1:], BF)

    @pl.when(row == rows_of - 1)
    def _():
        for k in range(cols_of):
            pix_out[k, RIM + tall : tall + 2 * RIM] = jnp.zeros((RIM, pix_ref.shape[1]), BF)
        up_out[UP_RIM + up_rows : up_rows + 2 * UP_RIM] = jnp.zeros((UP_RIM,) + up_ref.shape[1:], BF)

    own_pix.wait()
    own_up.wait()
    for k in range(1, cols_of):
        tile_copy(k).wait()
    for side, there in sides:

        @pl.when(there)
        def _():
            up_copy(side).wait_send()
            for k in range(cols_of):
                rim_copy(side, k).wait_send()

        other = not_last if side < 0 else not_first

        @pl.when(other)
        def _():
            up_copy(side).wait_recv()
            for k in range(cols_of):
                rim_copy(side, k).wait_recv()


def start(pix, up):
    rows_of, cols_of = lax.axis_size("row"), lax.axis_size("col")
    return pl.pallas_call(
        functools.partial(start_kernel, rows_of, cols_of),
        out_shape=(
            jax.ShapeDtypeStruct((cols_of, pix.shape[0] + 2 * RIM, pix.shape[1]), BF),
            jax.ShapeDtypeStruct((up.shape[0] + 2 * UP_RIM,) + up.shape[1:], BF),
        ),
        in_specs=[VMEM] * 2,
        out_specs=(VMEM, VMEM),
        scratch_shapes=[
            pltpu.SemaphoreType.DMA((4, cols_of)),
            pltpu.SemaphoreType.DMA((cols_of,)),
            pltpu.SemaphoreType.DMA((2, cols_of)),
            pltpu.SemaphoreType.DMA((2,)),
            pltpu.SemaphoreType.DMA((2,)),
        ],
        compiler_params=pltpu.CompilerParams(collective_id=0, has_side_effects=True),
    )(pix, up)


def sum_kernel(rows_of, count, *refs):
    ins, outs, held = refs[:count], refs[count : 2 * count], refs[2 * count : 3 * count]
    sends, recvs = refs[3 * count :]
    row, col = lax.axis_index("row"), lax.axis_index("col")
    barrier = pltpu.get_barrier_semaphore()
    for k in range(1, rows_of):
        pl.semaphore_signal(
            barrier, inc=1, device_id=(lax.rem(row + k, rows_of), col), device_id_type=MESH
        )
    pl.semaphore_wait(barrier, rows_of - 1)
    copies = []
    for k in range(1, rows_of):
        for n in range(count):
            copy = pltpu.make_async_remote_copy(
                src_ref=ins[n],
                dst_ref=held[n].at[row],
                send_sem=sends.at[n, k - 1],
                recv_sem=recvs.at[n, k - 1],
                device_id=(lax.rem(row + k, rows_of), col),
                device_id_type=MESH,
            )
            copy.start()
            copies.append(copy)
    for n in range(count):
        held[n][row] = ins[n][...]
    for copy in copies:
        copy.wait()
    for n in range(count):
        total = held[n][0].astype(F32)
        for k in range(1, rows_of):
            total = total + held[n][k].astype(F32)
        outs[n][...] = total


def row_sum_kernel(*parts):
    rows_of, count = lax.axis_size("row"), len(parts)
    return pl.pallas_call(
        functools.partial(sum_kernel, rows_of, count),
        out_shape=tuple(jax.ShapeDtypeStruct(part.shape, F32) for part in parts),
        in_specs=[VMEM] * count,
        out_specs=(VMEM,) * count,
        scratch_shapes=[pltpu.VMEM((rows_of,) + part.shape, BF) for part in parts]
        + [pltpu.SemaphoreType.DMA((count, rows_of - 1))] * 2,
        compiler_params=pltpu.CompilerParams(collective_id=1, has_side_effects=True),
    )(*parts)


def spread(field_ref, first, count, taps):
    _, cols, chans = field_ref.shape

    def one(r, carry):
        line = field_ref[first + r]
        wide = line.astype(F32)
        place = lax.broadcasted_iota(jnp.int32, (cols, chans), 0)
        before = jnp.where(place == 0, 0.0, pltpu.roll(wide, 1, 0)).astype(BF)
        after = jnp.where(place == cols - 1, 0.0, pltpu.roll(wide, cols - 1, 0)).astype(BF)
        taps[r] = jnp.concatenate([before, line, after], axis=1)
        return carry

    lax.fori_loop(0, count, one, 0)


def conv_kernel(halo, span, pre_from, backward, field_ref, kernel_ref, *refs):
    pre_ref, act_ref, taps = refs
    tall, cols, chans = field_ref.shape
    rows = tall - 2
    outs = kernel_ref.shape[2]
    step = 2
    spread(field_ref, 0, tall, taps)
    base = lax.axis_index("row") * (rows - 2 * halo) - halo

    def one(n, carry):
        r = n * step
        total = jnp.zeros((step * cols, outs), F32)
        for p in range(3):
            total = total + jnp.dot(
                taps[pl.ds(r + p, step)].reshape(step * cols, 3 * chans),
                kernel_ref[p],
                preferred_element_type=F32,
            )
        total = total.reshape(step, cols, outs)
        line = base + r + lax.broadcasted_iota(jnp.int32, (step, cols, outs), 0)
        inside = (line >= 0) & (line < span)
        if backward:
            pre = pre_ref[pl.ds(pre_from + r, step)]
            logistic = 1.0 / (1.0 + jnp.exp(-pre))
            value = total * (logistic * (1.0 + pre * (1.0 - logistic)))
        else:
            pre_ref[pl.ds(r, step)] = total
            value = total / (1.0 + jnp.exp(-total))
        act_ref[pl.ds(r, step)] = jnp.where(inside, value, 0.0).astype(BF)
        return carry

    lax.fori_loop(0, rows // step, one, 0)


def conv_call(field, kernel, halo, span, pre=None):
    tall, cols, chans = field.shape
    rows, outs = tall - 2, kernel.shape[3]
    backward = pre is not None
    pre_from = (pre.shape[0] - rows) // 2 if backward else 0
    shape = (rows, cols, outs)
    act = jax.ShapeDtypeStruct(shape, BF)
    ops = (field, kernel.reshape(3, 3 * chans, outs)) + ((pre,) if backward else ())
    return pl.pallas_call(
        functools.partial(conv_kernel, halo, span, pre_from, backward),
        out_shape=act if backward else (jax.ShapeDtypeStruct(shape, F32), act),
        in_specs=[VMEM] * len(ops),
        out_specs=VMEM if backward else (VMEM, VMEM),
        scratch_shapes=[pltpu.VMEM((tall, cols, 3 * chans), BF)],
        compiler_params=pltpu.CompilerParams(vmem_limit_bytes=48 * 1024 * 1024),
        cost_estimate=pl.CostEstimate(
            flops=18 * rows * cols * chans * outs, bytes_accessed=4 * rows * cols * outs, transcendentals=0
        ),
    )(*ops)


def grad_kernel(scale, field_from, delta_from, rows, field_ref, delta_ref, out_ref, taps):
    _, cols, chans = field_ref.shape
    outs = delta_ref.shape[2]
    spread(field_ref, field_from, rows + 2, taps)
    delta = delta_ref[delta_from : delta_from + rows].reshape(rows * cols, outs)
    for p in range(3):
        part = lax.dot_general(
            delta,
            taps[p : p + rows].reshape(rows * cols, 3 * chans),
            (((0,), (0,)), ((), ())),
            preferred_element_type=F32,
        )
        out_ref[p] = (part * scale).astype(BF)


def kernel_grad(field, delta, scale, rows):
    chans = field.shape[2]
    field_from, delta_from = (field.shape[0] - rows - 2) // 2, (delta.shape[0] - rows) // 2
    return pl.pallas_call(
        functools.partial(grad_kernel, scale, field_from, delta_from, rows),
        out_shape=jax.ShapeDtypeStruct((3, delta.shape[2], 3 * chans), BF),
        in_specs=[VMEM] * 2,
        out_specs=VMEM,
        scratch_shapes=[pltpu.VMEM((rows + 2, field.shape[1], 3 * chans), BF)],
        compiler_params=pltpu.CompilerParams(vmem_limit_bytes=48 * 1024 * 1024),
        cost_estimate=pl.CostEstimate(
            flops=18 * rows * field.shape[1] * chans * delta.shape[2], bytes_accessed=4 * delta.size, transcendentals=0
        ),
    )(field, delta)


def col_gather(block):
    return lax.all_gather(block, "col", axis=0)


def taps_last(part):
    chans = part.shape[2] // 3
    split = jnp.stack([part[:, :, q * chans : (q + 1) * chans] for q in range(3)], axis=1)
    return split.transpose(2, 3, 0, 1)


def forward_kernel(kernel):
    return kernel.transpose(2, 3, 1, 0)


def back_kernel(kernel):
    return jnp.flip(kernel, (2, 3)).transpose(2, 3, 0, 1)


def per_device(
    pixels, stem_weight, first_weight, second_weight, entry_weight, final_weight, upstream
):
    chans, pix_rows, pix_cols = pixels.shape
    rows, tile_cols = pix_rows // 2, pix_cols // 2
    row_count = lax.axis_size("row")
    col_count = lax.axis_size("col")
    cols = tile_cols * col_count
    group = upstream.shape[0]
    tail = group * col_count
    feats = stem_weight.shape[0]
    norm_scale = 1.0 / math.sqrt(rows * row_count * cols)
    base = lax.axis_index("row") * rows

    def inside(halo):
        pos = base - halo + jnp.arange(rows + 2 * halo)
        return ((pos >= 0) & (pos < rows * row_count))[:, None, None]

    def act(pre, halo):
        return jnp.where(inside(halo), jax.nn.silu(pre), 0.0).astype(BF)

    split = pixels.astype(BF).reshape(chans, pix_rows, tile_cols, 2)
    split = split.transpose(1, 0, 3, 2).reshape(pix_rows, chans * 2 * tile_cols)
    pix, up_own = start(split, upstream.transpose(1, 0, 2))
    order = lax.rem(lax.axis_index("col") - jnp.arange(col_count) + col_count, col_count)
    pix = jnp.take(pix[:, 3 : pix_rows + 2 * RIM - 3], order, axis=0)
    pix = pix.reshape(col_count, pix_rows + 26, chans, 2, tile_cols)
    pix = pix.transpose(2, 3, 1, 0, 4).reshape(chans, 2, pix_rows + 26, cols)
    weights = jnp.concatenate(
        [entry_weight.transpose(2, 3, 0, 1), final_weight.transpose(2, 3, 0, 1)], axis=3
    )
    weights = col_gather(weights).transpose(1, 2, 0, 3, 4).reshape(3, 3, tail, feats + tail)
    entry_all = weights[..., :feats].transpose(2, 3, 0, 1)
    final_all = weights[..., feats:].transpose(2, 3, 0, 1)
    up_all = col_gather(up_own)

    by_row = pix.reshape(chans, 2, rows + 13, 2, cols)
    padded = jnp.pad(by_row, ((0, 0),) * 4 + ((1, 1),))
    stem_rows = rows + 12
    taps = []
    for p in range(4):
        for q in range(4):
            odd, off = ((1, 0), (0, 1), (1, 1), (0, 2))[q]
            taps.append(
                padded[:, odd, p // 2 : p // 2 + stem_rows, p % 2, off : off + cols]
            )
    taps = jnp.stack(taps, axis=1).reshape(chans * 16, stem_rows, cols)
    stem_pre = lax.dot_general(
        taps.reshape(chans * 16, stem_rows * cols),
        stem_weight.reshape(feats, chans * 16),
        (((0,), (1,)), ((), ())),
        preferred_element_type=F32,
    ).reshape(stem_rows, cols, feats)
    stem_act = act(stem_pre, 6)
    span = rows * row_count
    first_pre, first_act = conv_call(stem_act, forward_kernel(first_weight), 5, span)
    second_pre, second_act = conv_call(first_act, forward_kernel(second_weight), 4, span)
    entry_pre, entry_act = conv_call(second_act, forward_kernel(entry_all), 3, span)

    final_part = kernel_grad(up_own.transpose(0, 2, 1), entry_act, norm_scale, rows)
    up_all = up_all.transpose(1, 3, 0, 2).reshape(rows + 2 * UP_RIM, cols, tail)

    entry_delta = conv_call(up_all, back_kernel(final_all), 3, span, entry_pre)
    own_delta = lax.dynamic_slice_in_dim(
        entry_delta, lax.axis_index("col") * group, group, axis=2
    )
    entry_part = kernel_grad(second_act, own_delta, norm_scale, rows)
    second_delta = conv_call(entry_delta, back_kernel(entry_all), 2, span, second_pre)
    second_part = kernel_grad(first_act, second_delta, norm_scale, rows)
    first_delta = conv_call(second_delta, back_kernel(second_weight), 1, span, first_pre)
    first_part = kernel_grad(stem_act, first_delta, norm_scale, rows)
    stem_delta = conv_call(first_delta, back_kernel(first_weight), 0, span, stem_pre)
    stem_part = lax.dot_general(
        stem_delta.reshape(rows * cols, feats),
        taps[:, 6:-6].reshape(chans * 16, rows * cols),
        (((0,), (1,)), ((), ())),
        preferred_element_type=F32,
    )
    stem_part = (stem_part * norm_scale).astype(BF)
    final_sum, stem_grad, first_grad, second_grad, entry_grad = row_sum_kernel(
        final_part, stem_part, first_part, second_part, entry_part
    )
    final_grad = jnp.flip(taps_last(final_sum), (2, 3)).transpose(1, 0, 2, 3)
    return (
        stem_grad.reshape(stem_weight.shape),
        taps_last(first_grad),
        taps_last(second_grad),
        taps_last(entry_grad),
        final_grad,
    )


def solution(mesh):
    return jax.shard_map(
        per_device,
        mesh=mesh,
        in_specs=(
            P(None, "row", "col"),
            P(),
            P(),
            P(),
            P("col", None, None, None),
            P("col", None, None, None),
            P("col", "row", None),
        ),
        out_specs=(P(), P(), P(), P("col", None, None, None), P("col", None, None, None)),
        check_vma=False,
    )
```

profile of v0, /device:TPU:0, one launch (start us, length us, event | category | flops | bytes accessed | tf_op | source)
XLA Modules:
  0.0 173.2 jit_solution(17304851424682386542)
XLA Ops:
  7.2 1.8 %pad_maximum_fusion = bf16[3,3,32,320]{3,2,1,0:T(8,128)(2,1)} fusion(bf16[3,3,32,256]{3,2,1,0:T(8,128)(2,1)} %bitcast.161, bf16[3,3,32,64]{3,2,1,0:T(8,128)(2,1)} %bitcast.164), kind=kLoop, calls=%fused_computation.20 | loop fusion | flops 368640 | bytes 368640 | tf_op jit(solution)/shard_map/concatenate | solution.py:343
  10.6 1.6 copy.631
  12.2 12.6 %shard_map.110 = (bf16[8,80,96]{2,1,0:T(8,128)(2,1)}, bf16[32,32,128]{2,1,0:T(8,128)(2,1)}) custom-call(bf16[48,96]{1,0:T(8,128)(2,1)} %copy.557.pix_ref, bf16[24,32,128]{2,1,0:T(8,128)(2,1)} %bitcast.156), custom_call_target="tpu_custom_call" | custom-call | tf_op jit(solution)/shard_map/pallas_call | solution.py:130
  33.1 2.4 %select_convert_fusion = (bf16[36,128,64]{2,1,0:T(8,128)(2,1)S(1)}, f32[36,128,64]{2,1,0:T(8,128)}) fusion(pred[36]{0:T(512)(128)(4,1)S(1)} %compare_and_fusion.1, bf16[64,48,1]{0,1,2:T(8,128)(2,1)S(1)} %bitcast.143, bf16[6,8,36,128]{3,2,1,0:T(8,128)(2,1)S(1)} %bitcast.160), kind=kOutput, calls=%fused_computation.1 | convolution fusion | flops 30081024 | bytes 2218020 | tf_op jit(solution)/shard_map/dot_general | solution.py:362
  35.5 7.4 %shard_map.111 = (f32[34,128,64]{2,1,0:T(8,128)S(1)}, bf16[34,128,64]{2,1,0:T(8,128)(2,1)S(1)}) custom-call(bf16[36,128,64]{2,1,0:T(8,128)(2,1)S(1)} %get-tuple-element.161.field_ref, bf16[3,192,64]{2,1,0:T(8,128)(2,1)S(1)} %bitcast.150), custom_call_target="tpu_custom_call" | custom-call | flops 320864256 | bytes 1114112 | tf_op jit(solution)/shard_map/pallas_call | solution.py:253
  44.4 7.1 %shard_map.112 = (f32[32,128,64]{2,1,0:T(8,128)S(1)}, bf16[32,128,64]{2,1,0:T(8,128)(2,1)S(1)}) custom-call(bf16[34,128,64]{2,1,0:T(8,128)(2,1)S(1)} %get-tuple-element.20.field_ref, bf16[3,192,64]{2,1,0:T(8,128)(2,1)S(1)} %bitcast.149), custom_call_target="tpu_custom_call" | custom-call | flops 301989888 | bytes 1048576 | tf_op jit(solution)/shard_map/pallas_call | solution.py:253
  53.8 3.0 %copy.567 = bf16[3,3,8,32,320]{4,3,2,1,0:T(8,128)(2,1)} copy(bf16[3,3,8,32,320]{4,3,1,0,2:T(8,128)(2,1)} %bitcast.154) | data formatting | bytes 2949120 | tf_op jit(solution)/shard_map/transpose | solution.py:346
  56.8 2.4 %slice_bitcast_fusion.1 = (bf16[256,64,3,3]{1,0,3,2:T(8,128)(2,1)}, bf16[3,3,64,256]{2,3,1,0:T(8,128)(2,1)}) fusion(bf16[3,3,256,320]{3,2,1,0:T(8,128)(2,1)} %bitcast.19), kind=kLoop, calls=%fused_computation.6 | loop fusion | bytes 884736 | tf_op jit(solution)/shard_map/transpose | solution.py:347
  59.1 2.0 %copy.568 = bf16[3,3,64,256]{3,2,1,0:T(8,128)(2,1)} copy(bf16[3,3,64,256]{2,3,1,0:T(8,128)(2,1)} %get-tuple-element.132) | data formatting | bytes 589824 | tf_op jit(solution)/shard_map/transpose;transpose | solution.py:308
  61.1 3.1 %slice_bitcast_fusion = bf16[256,256,3,3]{1,0,3,2:T(8,128)(2,1)} fusion(bf16[3,3,256,320]{3,2,1,0:T(8,128)(2,1)} %bitcast.19), kind=kLoop, calls=%fused_computation.2 | loop fusion | bytes 2359296 | tf_op jit(solution)/shard_map/transpose | solution.py:348
  64.2 2.4 %rev.19 = bf16[256,256,3,3]{1,0,3,2:T(8,128)(2,1)} reverse(bf16[256,256,3,3]{1,0,3,2:T(8,128)(2,1)} %slice_bitcast_fusion), dimensions={2,3} | reverse | bytes 2359296 | tf_op jit(solution)/shard_map/jit(_flip)/rev | solution.py:312
  66.6 2.0 %rev.20 = bf16[256,64,3,3]{1,0,3,2:T(8,128)(2,1)} reverse(bf16[256,64,3,3]{1,0,3,2:T(8,128)(2,1)} %get-tuple-element.131), dimensions={2,3} | reverse | bytes 589824 | tf_op jit(solution)/shard_map/jit(_flip)/rev | solution.py:312
  70.8 8.6 %shard_map.113 = (f32[30,128,256]{2,1,0:T(8,128)}, bf16[30,128,256]{2,1,0:T(8,128)(2,1)S(1)}) custom-call(bf16[32,128,64]{2,1,0:T(8,128)(2,1)S(1)} %copy-done.10, bf16[3,192,256]{2,1,0:T(8,128)(2,1)S(1)} %bitcast.151), custom_call_target="tpu_custom_call" | custom-call | flops 1132462080 | bytes 3932160 | tf_op jit(solution)/shard_map/pallas_call | solution.py:253
  79.4 3.7 %shard_map.114.refs_0_ = bf16[3,256,96]{2,1,0:T(8,128)(2,1)S(1)} custom-call(bf16[32,128,32]{2,1,0:T(8,128)(2,1)S(1)} %bitcast.144, bf16[30,128,256]{2,1,0:T(8,128)(2,1)S(1)} %get-tuple-element.22.delta_ref), custom_call_target="tpu_custom_call" | custom-call | flops 452984832 | bytes 3932160 | tf_op jit(solution)/shard_map/pallas_call | solution.py:284
  83.7 3.5 %copy.569 = bf16[32,128,8,32]{1,3,2,0:T(8,128)(2,1)} copy(bf16[32,128,8,32]{1,3,0,2:T(8,128)(2,1)} %bitcast.153) | data formatting | bytes 4194304 | tf_op jit(solution)/shard_map/transpose | solution.py:375
  87.2 4.2 %copy.570.field_ref = bf16[32,128,256]{2,1,0:T(8,128)(2,1)} copy(bf16[32,128,256]{1,2,0:T(8,128)(2,1)} %bitcast.152) | data formatting | bytes 4194304 | tf_op jit(solution)/shard_map/reshape | solution.py:375
  93.1 10.5 %shard_map.115.field_ref = bf16[30,128,256]{2,1,0:T(8,128)(2,1)S(1)} custom-call(bf16[32,128,256]{2,1,0:T(8,128)(2,1)S(1)} %copy-done.7, bf16[3,768,256]{2,1,0:T(8,128)(2,1)S(1)} %bitcast.146, f32[30,128,256]{2,1,0:T(8,128)} %get-tuple-element.23.refs_0_), custom_call_target="tpu_custom_call" | custom-call | flops 4529848320 | bytes 3932160 | tf_op jit(solution)/shard_map/pallas_call | solution.py:253
  103.6 7.4 %shard_map.116.field_ref.delta_ref = bf16[28,128,64]{2,1,0:T(8,128)(2,1)S(1)} custom-call(bf16[30,128,256]{2,1,0:T(8,128)(2,1)S(1)} %shard_map.115.field_ref, bf16[3,768,64]{2,1,0:T(8,128)(2,1)S(1)} %bitcast.145, f32[32,128,64]{2,1,0:T(8,128)S(1)} %copy-done.6), custom_call_target="tpu_custom_call" | custom-call | flops 1056964608 | bytes 917504 | tf_op jit(solution)/shard_map/pallas_call | solution.py:253
  111.0 3.0 %shard_map.120.refs_3_ = bf16[3,64,192]{2,1,0:T(8,128)(2,1)S(1)} custom-call(bf16[34,128,64]{2,1,0:T(8,128)(2,1)S(1)} %get-tuple-element.20.field_ref, bf16[28,128,64]{2,1,0:T(8,128)(2,1)S(1)} %shard_map.116.field_ref.delta_ref), custom_call_target="tpu_custom_call" | custom-call | flops 226492416 | bytes 917504 | tf_op jit(solution)/shard_map/pallas_call | solution.py:284
  114.7 5.5 %shard_map.117.field_ref.delta_ref = bf16[26,128,64]{2,1,0:T(8,128)(2,1)S(1)} custom-call(bf16[28,128,64]{2,1,0:T(8,128)(2,1)S(1)} %shard_map.116.field_ref.delta_ref, bf16[3,192,64]{2,1,0:T(8,128)(2,1)S(1)} %bitcast.148, f32[34,128,64]{2,1,0:T(8,128)S(1)} %copy-done.4), custom_call_target="tpu_custom_call" | custom-call | flops 245366784 | bytes 851968 | tf_op jit(solution)/shard_map/pallas_call | solution.py:253
  120.2 3.0 %shard_map.119.refs_2_ = bf16[3,64,192]{2,1,0:T(8,128)(2,1)S(1)} custom-call(bf16[36,128,64]{2,1,0:T(8,128)(2,1)S(1)} %get-tuple-element.161.field_ref, bf16[26,128,64]{2,1,0:T(8,128)(2,1)S(1)} %shard_map.117.field_ref.delta_ref), custom_call_target="tpu_custom_call" | custom-call | flops 226492416 | bytes 851968 | tf_op jit(solution)/shard_map/pallas_call | solution.py:284
  124.2 3.0 %shard_map.121.refs_4_ = bf16[3,32,192]{2,1,0:T(8,128)(2,1)S(1)} custom-call(bf16[32,128,64]{2,1,0:T(8,128)(2,1)S(1)} %copy-done.11, bf16[30,128,32]{2,1,0:T(8,128)(2,1)S(1)} %constant_dynamic-slice_fusion.delta_ref), custom_call_target="tpu_custom_call" | custom-call | flops 113246208 | bytes 491520 | tf_op jit(solution)/shard_map/pallas_call | solution.py:284
  127.3 5.1 %shard_map.118 = bf16[24,128,64]{2,1,0:T(8,128)(2,1)S(1)} custom-call(bf16[26,128,64]{2,1,0:T(8,128)(2,1)S(1)} %shard_map.117.field_ref.delta_ref, bf16[3,192,64]{2,1,0:T(8,128)(2,1)S(1)} %bitcast.147, f32[36,128,64]{2,1,0:T(8,128)S(1)} %copy-done.1), custom_call_target="tpu_custom_call" | custom-call | flops 226492416 | bytes 786432 | tf_op jit(solution)/shard_map/pallas_call | solution.py:253
  133.4 26.4 %shard_map.122 = (f32[3,256,96]{2,1,0:T(8,128)}, f32[64,48]{1,0:T(8,128)}, f32[3,64,192]{2,1,0:T(8,128)}, f32[3,64,192]{2,1,0:T(8,128)}, f32[3,32,192]{2,1,0:T(8,128)}) custom-call(bf16[3,256,96]{2,1,0:T(8,128)(2,1)} %copy-done.12, bf16[64,48]{1,0:T(8,128)(2,1)} %fusion.1.refs_1_, bf16[3,64,192]{2,1,0:T(8,128)(2,1)} %copy-done.17, ...), custom_call_target="tpu_custom_call" | custom-call | tf_op jit(solution)/shard_map/pallas_call | solution.py:185
  (113 shorter events, 27.0 us)
Async XLA Ops:
  7.2 26.0 %copy-start = (bf16[64,3,4,4]{0,3,2,1:T(4,128)(2,1)S(1)}, bf16[64,3,4,4]{0,3,2,1:T(4,128)(2,1)}, u32[]{:S(2)}) copy-start(bf16[64,3,4,4]{0,3,2,1:T(4,128)(2,1)} %param.8) | copy-start | bytes 18436
  7.2 46.6 %all-gather.5.cloned.1.call-start = ((), (), s32[]{:S(2)}) async-start(), calls=%async_computation | async-start | bytes 1990656 | tf_op jit(solution)/shard_map/all_gather | solution.py:298
  9.0 74.7 %all-gather.7.cloned.1.call-start = ((), (), s32[]{:S(2)}) async-start(), calls=%async_computation.1 | async-start | bytes 2359296 | tf_op jit(solution)/shard_map/all_gather | solution.py:298
  26.7 2.5 %copy-start.22 = (bf16[32,32,128]{2,1,0:T(8,128)(2,1)S(1)}, bf16[32,32,128]{2,1,0:T(8,128)(2,1)}, u32[]{:S(2)}) copy-start(bf16[32,32,128]{2,1,0:T(8,128)(2,1)} %get-tuple-element.18) | copy-start | bytes 786436
  29.2 1.6 copy-start.23
  29.2 3.1 %copy-start.24 = (bf16[64,64,3,3]{1,0,3,2:T(8,128)(2,1)S(1)}, bf16[64,64,3,3]{1,0,3,2:T(8,128)(2,1)}, u32[]{:S(2)}) copy-start(bf16[64,64,3,3]{1,0,3,2:T(8,128)(2,1)} %param.10) | copy-start | bytes 221188
  33.1 2.4 %copy-start.15 = (bf16[3,3,64,64]{3,2,1,0:T(8,128)(2,1)S(1)}, bf16[3,3,64,64]{3,2,1,0:T(8,128)(2,1)}, u32[]{:S(2)}) copy-start(bf16[3,3,64,64]{3,2,1,0:T(8,128)(2,1)} %copy.565) | copy-start | bytes 221188
  43.0 1.4 copy-start.3
  51.5 1.3 copy-start.5
  52.8 1.0 copy-start.9
  68.6 1.2 copy-start.10
  87.2 4.2 %copy-start.8 = (bf16[256,256,3,3]{1,0,3,2:T(8,128)(2,1)S(1)}, bf16[256,256,3,3]{1,0,3,2:T(8,128)(2,1)}, u32[]{:S(2)}) copy-start(bf16[256,256,3,3]{1,0,3,2:T(8,128)(2,1)} %rev.19) | copy-start | bytes 3538948
  91.5 1.6 copy-start.7
  93.1 10.5 %copy-start.2 = (bf16[256,64,3,3]{1,0,3,2:T(8,128)(2,1)S(1)}, bf16[256,64,3,3]{1,0,3,2:T(8,128)(2,1)}, u32[]{:S(2)}) copy-start(bf16[256,64,3,3]{1,0,3,2:T(8,128)(2,1)} %rev.20) | copy-start | bytes 884740
  93.1 10.5 %copy-start.6 = (f32[32,128,64]{2,1,0:T(8,128)S(1)}, f32[32,128,64]{2,1,0:T(8,128)}, u32[]{:S(2)}) copy-start(f32[32,128,64]{2,1,0:T(8,128)} %copy-done.5) | copy-start | bytes 3145732
  103.6 11.1 %copy-start.4 = (f32[34,128,64]{2,1,0:T(8,128)S(1)}, f32[34,128,64]{2,1,0:T(8,128)}, u32[]{:S(2)}) copy-start(f32[34,128,64]{2,1,0:T(8,128)} %copy-done.3) | copy-start | bytes 3342340
  111.0 3.7 %copy-start.14 = (bf16[64,64,3,3]{1,0,3,2:T(8,128)(2,1)S(1)}, bf16[64,64,3,3]{1,0,3,2:T(8,128)(2,1)}, u32[]{:S(2)}) copy-start(bf16[64,64,3,3]{1,0,3,2:T(8,128)(2,1)} %rev.21) | copy-start | bytes 221188
  120.2 4.0 %copy-start.11 = (bf16[32,128,64]{2,1,0:T(8,128)(2,1)S(1)}, bf16[32,128,64]{2,1,0:T(8,128)(2,1)}, u32[]{:S(2)}) copy-start(bf16[32,128,64]{2,1,0:T(8,128)(2,1)} %copy-done.9) | copy-start | bytes 1572868
  123.9 3.4 %copy-start.1 = (f32[36,128,64]{2,1,0:T(8,128)S(1)}, f32[36,128,64]{2,1,0:T(8,128)}, u32[]{:S(2)}) copy-start(f32[36,128,64]{2,1,0:T(8,128)} %get-tuple-element.162.refs_0_) | copy-start | bytes 3538948
  123.9 3.4 %copy-start.13 = (bf16[64,64,3,3]{1,0,3,2:T(8,128)(2,1)S(1)}, bf16[64,64,3,3]{1,0,3,2:T(8,128)(2,1)}, u32[]{:S(2)}) copy-start(bf16[64,64,3,3]{1,0,3,2:T(8,128)(2,1)} %rev.22) | copy-start | bytes 221188
  127.2 5.2 %copy-start.19 = (bf16[3,32,192]{2,1,0:T(8,128)(2,1)}, bf16[3,32,192]{2,1,0:T(8,128)(2,1)S(1)}, u32[]{:S(2)}) copy-start(bf16[3,32,192]{2,1,0:T(8,128)(2,1)S(1)} %shard_map.121.refs_4_) | copy-start | bytes 110596
  127.2 5.2 %copy-start.21 = (bf16[3,16,36,128]{3,1,0,2:T(8,128)(2,1)S(1)}, bf16[3,16,36,128]{3,1,0,2:T(8,128)(2,1)}, u32[]{:S(2)}) copy-start(bf16[3,16,36,128]{3,1,0,2:T(8,128)(2,1)} %copy.572) | copy-start | bytes 1327108
  159.8 4.3 %copy-start.25 = (f32[3,32,192]{2,1,0:T(8,128)S(1)}, f32[3,32,192]{2,1,0:T(8,128)}, u32[]{:S(2)}) copy-start(f32[3,32,192]{2,1,0:T(8,128)} %get-tuple-element.29) | copy-start | bytes 221188
  161.3 3.6 %copy-start.20 = (f32[3,256,96]{2,1,0:T(8,128)S(1)}, f32[3,256,96]{2,1,0:T(8,128)}, u32[]{:S(2)}) copy-start(f32[3,256,96]{2,1,0:T(8,128)} %get-tuple-element.30) | copy-start | bytes 884740
  (4 other events, 2.9 us)
Sparse Core Ops, SparseCore 0:
  10.2 29.2 all-gather.4
  41.1 28.9 all-gather.6
where the time goes:
time: 174 us; the launch traced here: 173 us
  Pallas kernels  103 us (59%)
  local copies, waits for them, and re-layouts  49 us (28%)
  between operations  14.6 us (8%)
  matrix products  3.41 us (2%)
  other arithmetic  2.8 us (2%)
    pallas_call x7, Pallas kernels, conv_call(): pl.pallas_call(functools.partial(conv_kernel, halo, span, pre_from, backw...  51.7 us
    pallas_call x1, Pallas kernels, row_sum_kernel(): pl.pallas_call(functools.partial(sum_kernel, rows_of, count), out_shape=t...  26.4 us
    unnamed x71, local copies, waits for them, and re-layouts  13.5 us
    pallas_call x4, Pallas kernels, kernel_grad(): pl.pallas_call(functools.partial(grad_kernel, scale, field_from, delta_fr...  12.6 us
    pallas_call x1, Pallas kernels, start(): pl.pallas_call(functools.partial(start_kernel, rows_of, cols_of), out_sha...  12.6 us
    rev x4, local copies, waits for them, and re-layouts, back_kernel(): return jnp.flip(kernel, (2, 3)).transpose(2, 3, 0, 1)  5.71 us
    reshape x1, local copies, waits for them, and re-layouts, per_device(): up_all = up_all.transpose(1, 3, 0, 2).reshape(rows + 2 * UP_RIM, cols, tail)  4.21 us
    transpose x1, local copies, waits for them, and re-layouts, per_device(): up_all = up_all.transpose(1, 3, 0, 2).reshape(rows + 2 * UP_RIM, cols, tail)  3.52 us
  transfers between devices with their start and end apart: 2, of which 0 were waited for; matrix products, arithmetic and copies ran while one was open for 16% of the time, Pallas kernels for 23%

commit v1 on v0

--- a/solution.py
+++ b/solution.py
@@ -16,6 +16,7 @@
 VMEM = pl.BlockSpec(memory_space=pltpu.VMEM)
 RIM = 16
 UP_RIM = 4
+UNROLL = 2
 
 
 def start_kernel(rows_of, cols_of, pix_ref, up_ref, pix_out, up_out, sends, pix_recv, rim_recv, up_recv, own_sems):
@@ -147,8 +148,9 @@
 
 
 def sum_kernel(rows_of, count, *refs):
-    ins, outs, held = refs[:count], refs[count : 2 * count], refs[2 * count : 3 * count]
-    sends, recvs = refs[3 * count :]
+    ins, outs = refs[:count], refs[count : 2 * count]
+    held, mine = refs[2 * count : 3 * count], refs[3 * count : 4 * count]
+    sends, recvs = refs[4 * count :]
     row, col = lax.axis_index("row"), lax.axis_index("col")
     barrier = pltpu.get_barrier_semaphore()
     for k in range(1, rows_of):
@@ -156,65 +158,79 @@
             barrier, inc=1, device_id=(lax.rem(row + k, rows_of), col), device_id_type=MESH
         )
     pl.semaphore_wait(barrier, rows_of - 1)
-    copies = []
-    for k in range(1, rows_of):
-        for n in range(count):
-            copy = pltpu.make_async_remote_copy(
-                src_ref=ins[n],
-                dst_ref=held[n].at[row],
-                send_sem=sends.at[n, k - 1],
-                recv_sem=recvs.at[n, k - 1],
-                device_id=(lax.rem(row + k, rows_of), col),
-                device_id_type=MESH,
-            )
-            copy.start()
-            copies.append(copy)
+
+    def copy(stage, n, k):
+        peer = lax.rem(row + k, rows_of)
+        return pltpu.make_async_remote_copy(
+            src_ref=ins[n].at[peer] if stage == 0 else mine[n],
+            dst_ref=held[n].at[k - 1] if stage == 0 else outs[n].at[row],
+            send_sem=sends.at[stage, n, k - 1],
+            recv_sem=recvs.at[stage, n, k - 1],
+            device_id=(peer, col),
+            device_id_type=MESH,
+        )
+
     for n in range(count):
-        held[n][row] = ins[n][...]
-    for copy in copies:
-        copy.wait()
+        for k in range(1, rows_of):
+            copy(0, n, k).start()
     for n in range(count):
-        total = held[n][0].astype(F32)
+        total = ins[n][row].astype(F32)
         for k in range(1, rows_of):
-            total = total + held[n][k].astype(F32)
-        outs[n][...] = total
+            copy(0, n, k).wait_recv()
+            total = total + held[n][k - 1].astype(F32)
+        mine[n][...] = total.astype(BF)
+        outs[n][row] = total.astype(BF)
+        for k in range(1, rows_of):
+            copy(1, n, k).start()
+    for n in range(count):
+        for k in range(1, rows_of):
+            copy(0, n, k).wait_send()
+            copy(1, n, k).wait()
 
 
 def row_sum_kernel(*parts):
     rows_of, count = lax.axis_size("row"), len(parts)
-    return pl.pallas_call(
+    cut = [part.reshape(rows_of, -1, part.shape[-1]) for part in parts]
+    sums = pl.pallas_call(
         functools.partial(sum_kernel, rows_of, count),
-        out_shape=tuple(jax.ShapeDtypeStruct(part.shape, F32) for part in parts),
+        out_shape=tuple(jax.ShapeDtypeStruct(part.shape, BF) for part in cut),
         in_specs=[VMEM] * count,
         out_specs=(VMEM,) * count,
-        scratch_shapes=[pltpu.VMEM((rows_of,) + part.shape, BF) for part in parts]
-        + [pltpu.SemaphoreType.DMA((count, rows_of - 1))] * 2,
+        scratch_shapes=[pltpu.VMEM((rows_of - 1,) + part.shape[1:], BF) for part in cut]
+        + [pltpu.VMEM(part.shape[1:], BF) for part in cut]
+        + [pltpu.SemaphoreType.DMA((2, count, rows_of - 1))] * 2,
         compiler_params=pltpu.CompilerParams(collective_id=1, has_side_effects=True),
-    )(*parts)
-
-
-def spread(field_ref, first, count, taps):
-    _, cols, chans = field_ref.shape
+    )(*cut)
+    return [total.reshape(part.shape).astype(F32) for total, part in zip(sums, parts)]
+
+
+def spread(field_ref, first, count, taps, backward=False):
+    cols, chans = taps.shape[1], taps.shape[2] // 3
 
     def one(r, carry):
-        line = field_ref[first + r]
-        wide = line.astype(F32)
+        if len(field_ref.shape) == 4:
+            groups = [field_ref[g, first + r] for g in range(field_ref.shape[0])]
+            wide = jnp.concatenate(groups, axis=0).astype(F32).T
+            line = wide.astype(BF)
+        else:
+            line = field_ref[first + r]
+            wide = line.astype(F32)
         place = lax.broadcasted_iota(jnp.int32, (cols, chans), 0)
         before = jnp.where(place == 0, 0.0, pltpu.roll(wide, 1, 0)).astype(BF)
         after = jnp.where(place == cols - 1, 0.0, pltpu.roll(wide, cols - 1, 0)).astype(BF)
-        taps[r] = jnp.concatenate([before, line, after], axis=1)
+        near = [after, line, before] if backward else [before, line, after]
+        taps[r] = jnp.concatenate(near, axis=1)
         return carry
 
-    lax.fori_loop(0, count, one, 0)
-
-
-def conv_kernel(halo, span, pre_from, backward, field_ref, kernel_ref, *refs):
+    lax.fori_loop(0, count, one, 0, unroll=2)
+
+
+def conv_kernel(halo, span, pre_from, backward, first, field_ref, kernel_ref, *refs):
     pre_ref, act_ref, taps = refs
-    tall, cols, chans = field_ref.shape
-    rows = tall - 2
-    outs = kernel_ref.shape[2]
+    tall, cols, wide = taps.shape
+    rows, outs = tall - 2, act_ref.shape[2]
     step = 2
-    spread(field_ref, 0, tall, taps)
+    spread(field_ref, 0, tall, taps, backward)
     base = lax.axis_index("row") * (rows - 2 * halo) - halo
 
     def one(n, carry):
@@ -222,8 +238,8 @@
         total = jnp.zeros((step * cols, outs), F32)
         for p in range(3):
             total = total + jnp.dot(
-                taps[pl.ds(r + p, step)].reshape(step * cols, 3 * chans),
-                kernel_ref[p],
+                taps[pl.ds(r + p, step)].reshape(step * cols, wide),
+                kernel_ref[2 - p if backward else p, :, first : first + outs],
                 preferred_element_type=F32,
             )
         total = total.reshape(step, cols, outs)
@@ -239,19 +255,22 @@
         act_ref[pl.ds(r, step)] = jnp.where(inside, value, 0.0).astype(BF)
         return carry
 
-    lax.fori_loop(0, rows // step, one, 0)
-
-
-def conv_call(field, kernel, halo, span, pre=None):
-    tall, cols, chans = field.shape
-    rows, outs = tall - 2, kernel.shape[3]
+    lax.fori_loop(0, rows // step, one, 0, unroll=UNROLL)
+
+
+def conv_call(field, kernel, halo, span, pre=None, first=0, outs=None):
+    if field.ndim == 4:
+        tall, cols, chans = field.shape[1], field.shape[3], field.shape[0] * field.shape[2]
+    else:
+        tall, cols, chans = field.shape
+    rows, outs = tall - 2, outs or kernel.shape[3]
     backward = pre is not None
     pre_from = (pre.shape[0] - rows) // 2 if backward else 0
     shape = (rows, cols, outs)
     act = jax.ShapeDtypeStruct(shape, BF)
-    ops = (field, kernel.reshape(3, 3 * chans, outs)) + ((pre,) if backward else ())
+    ops = (field, kernel.reshape(3, 3 * chans, kernel.shape[3])) + ((pre,) if backward else ())
     return pl.pallas_call(
-        functools.partial(conv_kernel, halo, span, pre_from, backward),
+        functools.partial(conv_kernel, halo, span, pre_from, backward, first),
         out_shape=act if backward else (jax.ShapeDtypeStruct(shape, F32), act),
         in_specs=[VMEM] * len(ops),
         out_specs=VMEM if backward else (VMEM, VMEM),
@@ -309,7 +328,7 @@
 
 
 def back_kernel(kernel):
-    return jnp.flip(kernel, (2, 3)).transpose(2, 3, 0, 1)
+    return kernel.transpose(2, 3, 0, 1)
 
 
 def per_device(
@@ -340,12 +359,9 @@
     pix = jnp.take(pix[:, 3 : pix_rows + 2 * RIM - 3], order, axis=0)
     pix = pix.reshape(col_count, pix_rows + 26, chans, 2, tile_cols)
     pix = pix.transpose(2, 3, 1, 0, 4).reshape(chans, 2, pix_rows + 26, cols)
-    weights = jnp.concatenate(
-        [entry_weight.transpose(2, 3, 0, 1), final_weight.transpose(2, 3, 0, 1)], axis=3
-    )
-    weights = col_gather(weights).transpose(1, 2, 0, 3, 4).reshape(3, 3, tail, feats + tail)
-    entry_all = weights[..., :feats].transpose(2, 3, 0, 1)
-    final_all = weights[..., feats:].transpose(2, 3, 0, 1)
+    weights = jnp.concatenate([back_kernel(final_weight), back_kernel(entry_weight)], axis=3)
+    weights = col_gather(weights).transpose(1, 2, 0, 3, 4).reshape(3, 3, tail, tail + feats)
+    entry_forward = weights[..., tail:].transpose(0, 1, 3, 2)
     up_all = col_gather(up_own)
 
     by_row = pix.reshape(chans, 2, rows + 13, 2, cols)
@@ -369,17 +385,15 @@
     span = rows * row_count
     first_pre, first_act = conv_call(stem_act, forward_kernel(first_weight), 5, span)
     second_pre, second_act = conv_call(first_act, forward_kernel(second_weight), 4, span)
-    entry_pre, entry_act = conv_call(second_act, forward_kernel(entry_all), 3, span)
+    entry_pre, entry_act = conv_call(second_act, entry_forward, 3, span)
 
     final_part = kernel_grad(up_own.transpose(0, 2, 1), entry_act, norm_scale, rows)
-    up_all = up_all.transpose(1, 3, 0, 2).reshape(rows + 2 * UP_RIM, cols, tail)
-
-    entry_delta = conv_call(up_all, back_kernel(final_all), 3, span, entry_pre)
+    entry_delta = conv_call(up_all, weights, 3, span, entry_pre, 0, tail)
     own_delta = lax.dynamic_slice_in_dim(
         entry_delta, lax.axis_index("col") * group, group, axis=2
     )
     entry_part = kernel_grad(second_act, own_delta, norm_scale, rows)
-    second_delta = conv_call(entry_delta, back_kernel(entry_all), 2, span, second_pre)
+    second_delta = conv_call(entry_delta, weights, 2, span, second_pre, tail, feats)
     second_part = kernel_grad(first_act, second_delta, norm_scale, rows)
     first_delta = conv_call(second_delta, back_kernel(second_weight), 1, span, first_pre)
     first_part = kernel_grad(stem_act, first_delta, norm_scale, rows)

time: 174 us -> 138 us (0.79)
  Pallas kernels: 103 us -> 79.2 us
  local copies, waits for them, and re-layouts: 49 us -> 29.2 us
  waiting for transfers between devices: 0.04 us -> 4.99 us
  other arithmetic: 2.8 us -> 6.78 us
    transpose x4 -> x0, local copies, waits for them, and re-layouts: 11.9 us -> none  [the longest x1 3.52 us: per_device(): up_all = up_all.transpose(1, 3, 0, 2).reshape(rows + 2 * UP_RIM, cols, tail)]
    pallas_call x1, Pallas kernels: 26.4 us -> 16 us  [row_sum_kernel(): pl.pallas_call(functools.partial(sum_kernel, rows_of, count), out_shape=t...]
    pallas_call x7, Pallas kernels: 51.7 us -> 41.5 us  [conv_call(): pl.pallas_call(functools.partial(conv_kernel, halo, span, pre_from, backw...]
    rev x4 -> x0, local copies, waits for them, and re-layouts: 5.71 us -> none  [back_kernel(): return jnp.flip(kernel, (2, 3)).transpose(2, 3, 0, 1)]
    all_gather x2, waiting for transfers between devices: 0.01 us -> 4.96 us  [col_gather(): return lax.all_gather(block, 'col', axis=0)]
    reshape x1 -> x0, local copies, waits for them, and re-layouts: 4.21 us -> none  [per_device(): up_all = up_all.transpose(1, 3, 0, 2).reshape(rows + 2 * UP_RIM, cols, tail)]
    pallas_call x4, Pallas kernels: 12.6 us -> 9.07 us  [kernel_grad(): pl.pallas_call(functools.partial(grad_kernel, scale, field_from, delta_fr...]
    convert_element_type x0 -> x3, other arithmetic: none -> 2.63 us  [row_sum_kernel(): total.reshape(part.shape).astype(F32)]
  transfers between devices with their start and end apart: 2 -> 2, of which waited for: 0 -> 1; matrix products, arithmetic and copies ran while one was open for 16% -> 13% of each run, Pallas kernels for 23% -> 23%
where the time goes in v1:
time: 138 us; the launch traced here: 137 us
  Pallas kernels  79.2 us (57%)
  local copies, waits for them, and re-layouts  29.2 us (21%)
  between operations  14.5 us (11%)
  other arithmetic  6.78 us (5%)
  waiting for transfers between devices  4.99 us (4%)
  matrix products  2.64 us (2%)
    pallas_call x7, Pallas kernels, conv_call(): pl.pallas_call(functools.partial(conv_kernel, halo, span, pre_from, backw...  41.5 us
    pallas_call x1, Pallas kernels, row_sum_kernel(): pl.pallas_call(functools.partial(sum_kernel, rows_of, count), out_shape=t...  16 us
    unnamed x64, local copies, waits for them, and re-layouts  14.6 us
    pallas_call x1, Pallas kernels, start(): pl.pallas_call(functools.partial(start_kernel, rows_of, cols_of), out_sha...  12.6 us
    pallas_call x4, Pallas kernels, kernel_grad(): pl.pallas_call(functools.partial(grad_kernel, scale, field_from, delta_fr...  9.07 us
    all_gather x2, waiting for transfers between devices, col_gather(): return lax.all_gather(block, 'col', axis=0)  4.96 us
  transfers between devices with their start and end apart: 2, of which 1 were waited for; matrix products, arithmetic and copies ran while one was open for 13% of the time, Pallas kernels for 23%

profile of v1, /device:TPU:0, one launch (start us, length us, event | category | flops | bytes accessed | tf_op | source)
XLA Modules:
  0.0 137.4 jit_solution(16086122994425781214)
XLA Ops:
  7.2 1.7 %pad_maximum_fusion = bf16[3,3,32,320]{3,2,1,0:T(8,128)(2,1)} fusion(bf16[3,3,32,64]{3,2,1,0:T(8,128)(2,1)} %bitcast.187, bf16[3,3,32,256]{3,2,1,0:T(8,128)(2,1)} %bitcast.182), kind=kLoop, calls=%fused_computation.13 | loop fusion | flops 368640 | bytes 368640 | tf_op jit(solution)/shard_map/concatenate | solution.py:362
  10.5 1.6 %copy.632 = bf16[32,24,128]{2,0,1:T(8,128)(2,1)} copy(bf16[32,24,128]{2,1,0:T(8,128)(2,1)} %param.13) | data formatting | bytes 393216 | tf_op args[6]
  12.1 12.6 %shard_map.110 = (bf16[8,80,96]{2,1,0:T(8,128)(2,1)}, bf16[32,32,128]{2,1,0:T(8,128)(2,1)}) custom-call(bf16[48,96]{1,0:T(8,128)(2,1)} %copy.556.pix_ref, bf16[24,32,128]{2,1,0:T(8,128)(2,1)} %bitcast.176), custom_call_target="tpu_custom_call" | custom-call | tf_op jit(solution)/shard_map/pallas_call | solution.py:131
  24.8 2.3 %copy.557 = bf16[32,32,128]{1,2,0:T(8,128)(2,1)} copy(bf16[32,32,128]{2,1,0:T(8,128)(2,1)} %get-tuple-element.18) | data formatting | bytes 524288 | tf_op jit(solution)/shard_map/pallas_call | solution.py:131
  32.8 2.4 %select_convert_fusion = (bf16[36,128,64]{2,1,0:T(8,128)(2,1)S(1)}, f32[36,128,64]{2,1,0:T(8,128)}) fusion(pred[36]{0:T(512)(128)(4,1)S(1)} %compare_and_fusion.1, bf16[64,48,1]{0,1,2:T(8,128)(2,1)S(1)} %bitcast.156, bf16[6,8,36,128]{3,2,1,0:T(8,128)(2,1)S(1)} %bitcast.178), kind=kOutput, calls=%fused_computation.1 | convolution fusion | flops 30081024 | bytes 2218020 | tf_op jit(solution)/shard_map/dot_general | solution.py:378
  35.2 4.9 %shard_map.111 = (f32[34,128,64]{2,1,0:T(8,128)S(1)}, bf16[34,128,64]{2,1,0:T(8,128)(2,1)S(1)}) custom-call(bf16[36,128,64]{2,1,0:T(8,128)(2,1)S(1)} %get-tuple-element.64.field_ref, bf16[3,192,64]{2,1,0:T(8,128)(2,1)S(1)} %bitcast.167), custom_call_target="tpu_custom_call" | custom-call | flops 320864256 | bytes 1114112 | tf_op jit(solution)/shard_map/pallas_call | solution.py:272
  40.1 1.4 %copy-done.7 = f32[34,128,64]{2,1,0:T(8,128)} copy-done((f32[34,128,64]{2,1,0:T(8,128)}, f32[34,128,64]{2,1,0:T(8,128)S(1)}, u32[]{:S(2)}) %copy-start.7) | copy-done | bytes 1114136
  41.5 4.5 %shard_map.112 = (f32[32,128,64]{2,1,0:T(8,128)S(1)}, bf16[32,128,64]{2,1,0:T(8,128)(2,1)S(1)}) custom-call(bf16[34,128,64]{2,1,0:T(8,128)(2,1)S(1)} %get-tuple-element.20.field_ref, bf16[3,192,64]{2,1,0:T(8,128)(2,1)S(1)} %bitcast.166), custom_call_target="tpu_custom_call" | custom-call | flops 301989888 | bytes 1048576 | tf_op jit(solution)/shard_map/pallas_call | solution.py:272
  47.0 1.4 %copy-done.9 = f32[32,128,64]{2,1,0:T(8,128)} copy-done((f32[32,128,64]{2,1,0:T(8,128)}, f32[32,128,64]{2,1,0:T(8,128)S(1)}, u32[]{:S(2)}) %copy-start.9) | copy-done | bytes 1048600
  49.4 1.7 %copy.566 = bf16[8,3,3,32,320]{4,3,0,2,1:T(8,128)(2,1)S(1)} copy(bf16[8,3,3,32,320]{4,3,2,1,0:T(8,128)(2,1)} %bitcast.175) | data formatting | bytes 2949120 | tf_op jit(solution)/shard_map/all_gather | solution.py:317
  53.4 1.3 copy-done.11
  54.7 6.6 %shard_map.113 = (f32[30,128,256]{2,1,0:T(8,128)}, bf16[30,128,256]{2,1,0:T(8,128)(2,1)S(1)}) custom-call(bf16[32,128,64]{2,1,0:T(8,128)(2,1)S(1)} %copy-done.11, bf16[3,192,256]{2,1,0:T(8,128)(2,1)S(1)} %bitcast.170), custom_call_target="tpu_custom_call" | custom-call | flops 1132462080 | bytes 3932160 | tf_op jit(solution)/shard_map/pallas_call | solution.py:272
  61.3 2.8 %shard_map.114 = bf16[3,256,96]{2,1,0:T(8,128)(2,1)S(1)} custom-call(bf16[32,128,32]{2,1,0:T(8,128)(2,1)S(1)} %bitcast.160, bf16[30,128,256]{2,1,0:T(8,128)(2,1)S(1)} %get-tuple-element.22.delta_ref), custom_call_target="tpu_custom_call" | custom-call | flops 452984832 | bytes 3932160 | tf_op jit(solution)/shard_map/pallas_call | solution.py:303
  64.8 5.0 %all-gather.7.cloned.1.call-done = bf16[256,32,128]{2,1,0:T(8,128)(2,1)} async-done(((bf16[32,32,128]{2,1,0:T(8,128)(2,1)}), bf16[256,32,128]{2,1,0:T(8,128)(2,1)}) %all-gather.7.cloned.1.call-update) | async-done | bytes 2097168 | tf_op jit(solution)/shard_map/all_gather | solution.py:317
  69.7 1.6 %copy-done.19 = bf16[256,32,128]{2,1,0:T(8,128)(2,1)S(1)} copy-done((bf16[256,32,128]{2,1,0:T(8,128)(2,1)S(1)}, bf16[256,32,128]{2,1,0:T(8,128)(2,1)}, u32[]{:S(2)}) %copy-start.19) | copy-done | bytes 2097176
  71.3 10.6 %shard_map.115.field_ref = bf16[30,128,256]{2,1,0:T(8,128)(2,1)S(1)} custom-call(bf16[8,32,32,128]{3,2,1,0:T(8,128)(2,1)S(1)} %bitcast.172, bf16[3,768,320]{2,1,0:T(8,128)(2,1)S(1)} %bitcast.158, f32[30,128,256]{2,1,0:T(8,128)} %get-tuple-element.23.refs_0_), custom_call_target="tpu_custom_call" | custom-call | flops 4529848320 | bytes 3932160 | tf_op jit(solution)/shard_map/pallas_call | solution.py:272
  81.9 8.0 %shard_map.116.field_ref.delta_ref = bf16[28,128,64]{2,1,0:T(8,128)(2,1)S(1)} custom-call(bf16[30,128,256]{2,1,0:T(8,128)(2,1)S(1)} %shard_map.115.field_ref, bf16[3,768,320]{2,1,0:T(8,128)(2,1)S(1)} %bitcast.159, f32[32,128,64]{2,1,0:T(8,128)} %copy-done.9), custom_call_target="tpu_custom_call" | custom-call | flops 1056964608 | bytes 917504 | tf_op jit(solution)/shard_map/pallas_call | solution.py:272
  89.9 1.3 copy-done.3
  91.2 2.1 %shard_map.120 = bf16[3,64,192]{2,1,0:T(8,128)(2,1)S(1)} custom-call(bf16[34,128,64]{2,1,0:T(8,128)(2,1)S(1)} %copy-done.2, bf16[28,128,64]{2,1,0:T(8,128)(2,1)S(1)} %shard_map.116.field_ref.delta_ref), custom_call_target="tpu_custom_call" | custom-call | flops 226492416 | bytes 917504 | tf_op jit(solution)/shard_map/pallas_call | solution.py:303
  93.4 3.6 %shard_map.117.field_ref.delta_ref = bf16[26,128,64]{2,1,0:T(8,128)(2,1)S(1)} custom-call(bf16[28,128,64]{2,1,0:T(8,128)(2,1)S(1)} %shard_map.116.field_ref.delta_ref, bf16[3,192,64]{2,1,0:T(8,128)(2,1)S(1)} %bitcast.163, f32[34,128,64]{2,1,0:T(8,128)S(1)} %copy-done.8), custom_call_target="tpu_custom_call" | custom-call | flops 245366784 | bytes 851968 | tf_op jit(solution)/shard_map/pallas_call | solution.py:272
  97.0 2.1 %shard_map.119 = bf16[3,64,192]{2,1,0:T(8,128)(2,1)S(1)} custom-call(bf16[36,128,64]{2,1,0:T(8,128)(2,1)S(1)} %get-tuple-element.64.field_ref, bf16[26,128,64]{2,1,0:T(8,128)(2,1)S(1)} %shard_map.117.field_ref.delta_ref), custom_call_target="tpu_custom_call" | custom-call | flops 226492416 | bytes 851968 | tf_op jit(solution)/shard_map/pallas_call | solution.py:303
  99.8 3.3 %shard_map.118 = bf16[24,128,64]{2,1,0:T(8,128)(2,1)S(1)} custom-call(bf16[26,128,64]{2,1,0:T(8,128)(2,1)S(1)} %shard_map.117.field_ref.delta_ref, bf16[3,192,64]{2,1,0:T(8,128)(2,1)S(1)} %bitcast.165, f32[36,128,64]{2,1,0:T(8,128)S(1)} %copy-done.6), custom_call_target="tpu_custom_call" | custom-call | flops 226492416 | bytes 786432 | tf_op jit(solution)/shard_map/pallas_call | solution.py:272
  104.4 2.1 %shard_map.121 = bf16[3,32,192]{2,1,0:T(8,128)(2,1)S(1)} custom-call(bf16[32,128,64]{2,1,0:T(8,128)(2,1)S(1)} %copy-done.12, bf16[30,128,32]{2,1,0:T(8,128)(2,1)S(1)} %constant_dynamic-slice_fusion.delta_ref), custom_call_target="tpu_custom_call" | custom-call | flops 113246208 | bytes 491520 | tf_op jit(solution)/shard_map/pallas_call | solution.py:303
  107.2 16.0 %shard_map.122 = (bf16[4,192,96]{2,1,0:T(8,128)(2,1)}, bf16[4,16,48]{2,1,0:T(8,128)(2,1)}, bf16[4,48,192]{2,1,0:T(8,128)(2,1)}, bf16[4,48,192]{2,1,0:T(8,128)(2,1)}, bf16[4,24,192]{2,1,0:T(8,128)(2,1)}) custom-call(bf16[4,192,96]{2,1,0:T(8,128)(2,1)} %bitcast.161, bf16[4,16,48]{2,1,0:T(8,128)(2,1)} %bitcast.188, bf16[4,48,192]{2,1,0:T(8,128)(2,1)} %bitcast.169, ...), custom_call_target="tpu_custom_call" | custom-call | tf_op jit(solution)/shard_map/pallas_call | solution.py:194
  (100 shorter events, 22.0 us)
Async XLA Ops:
  7.2 25.6 %copy-start = (bf16[64,3,4,4]{0,3,2,1:T(4,128)(2,1)S(1)}, bf16[64,3,4,4]{0,3,2,1:T(4,128)(2,1)}, u32[]{:S(2)}) copy-start(bf16[64,3,4,4]{0,3,2,1:T(4,128)(2,1)} %param.8) | copy-start | bytes 18436
  7.2 42.2 %all-gather.5.cloned.1.call-start = ((), (), s32[]{:S(2)}) async-start(), calls=%async_computation | async-start | bytes 1990656 | tf_op jit(solution)/shard_map/all_gather | solution.py:317
  8.9 60.8 %all-gather.7.cloned.1.call-start = ((), (), s32[]{:S(2)}) async-start(), calls=%async_computation.1 | async-start | bytes 2359296 | tf_op jit(solution)/shard_map/all_gather | solution.py:317
  30.4 2.1 %copy-start.15 = (bf16[64,64,3,3]{1,0,3,2:T(8,128)(2,1)S(1)}, bf16[64,64,3,3]{1,0,3,2:T(8,128)(2,1)}, u32[]{:S(2)}) copy-start(bf16[64,64,3,3]{1,0,3,2:T(8,128)(2,1)} %param.9) | copy-start | bytes 221188
  30.6 2.0 %copy-start.14 = (bf16[64,64,3,3]{1,0,3,2:T(8,128)(2,1)S(1)}, bf16[64,64,3,3]{1,0,3,2:T(8,128)(2,1)}, u32[]{:S(2)}) copy-start(bf16[64,64,3,3]{1,0,3,2:T(8,128)(2,1)} %param.10) | copy-start | bytes 221188
  40.1 1.4 %copy-start.7 = (f32[34,128,64]{2,1,0:T(8,128)}, f32[34,128,64]{2,1,0:T(8,128)S(1)}, u32[]{:S(2)}) copy-start(f32[34,128,64]{2,1,0:T(8,128)S(1)} %get-tuple-element.25.refs_0_) | copy-start | bytes 3342340
  46.0 1.0 copy-start.1
  47.0 1.4 %copy-start.9 = (f32[32,128,64]{2,1,0:T(8,128)}, f32[32,128,64]{2,1,0:T(8,128)S(1)}, u32[]{:S(2)}) copy-start(f32[32,128,64]{2,1,0:T(8,128)S(1)} %get-tuple-element.24.refs_0_) | copy-start | bytes 3145732
  48.4 1.0 copy-start.10
  53.4 8.0 %copy-start.5 = (bf16[32,32,128]{1,2,0:T(8,128)(2,1)S(1)}, bf16[32,32,128]{1,2,0:T(8,128)(2,1)}, u32[]{:S(2)}) copy-start(bf16[32,32,128]{1,2,0:T(8,128)(2,1)} %copy.557) | copy-start | bytes 786436
  53.4 1.3 copy-start.11
  64.1 0.7 copy-start.13
  69.7 1.6 %copy-start.19 = (bf16[256,32,128]{2,1,0:T(8,128)(2,1)S(1)}, bf16[256,32,128]{2,1,0:T(8,128)(2,1)}, u32[]{:S(2)}) copy-start(bf16[256,32,128]{2,1,0:T(8,128)(2,1)} %all-gather.7.cloned.1.call-done) | copy-start | bytes 6291460
  81.9 9.4 %copy-start.2 = (bf16[34,128,64]{2,1,0:T(8,128)(2,1)S(1)}, bf16[34,128,64]{2,1,0:T(8,128)(2,1)}, u32[]{:S(2)}) copy-start(bf16[34,128,64]{2,1,0:T(8,128)(2,1)} %copy-done.1) | copy-start | bytes 1671172
  81.9 11.5 %copy-start.8 = (f32[34,128,64]{2,1,0:T(8,128)S(1)}, f32[34,128,64]{2,1,0:T(8,128)}, u32[]{:S(2)}) copy-start(f32[34,128,64]{2,1,0:T(8,128)} %copy-done.7) | copy-start | bytes 3342340
  89.9 1.3 copy-start.3
  93.4 5.8 %copy-start.16 = (bf16[3,64,192]{2,1,0:T(8,128)(2,1)}, bf16[3,64,192]{2,1,0:T(8,128)(2,1)S(1)}, u32[]{:S(2)}) copy-start(bf16[3,64,192]{2,1,0:T(8,128)(2,1)S(1)} %shard_map.120) | copy-start | bytes 221188
  93.4 6.4 %copy-start.6 = (f32[36,128,64]{2,1,0:T(8,128)S(1)}, f32[36,128,64]{2,1,0:T(8,128)}, u32[]{:S(2)}) copy-start(f32[36,128,64]{2,1,0:T(8,128)} %get-tuple-element.65.refs_0_) | copy-start | bytes 3538948
  99.1 0.6 copy-start.17
  99.8 3.3 %copy-start.21 = (bf16[3,16,36,128]{3,1,0,2:T(8,128)(2,1)S(1)}, bf16[3,16,36,128]{3,1,0,2:T(8,128)(2,1)}, u32[]{:S(2)}) copy-start(bf16[3,16,36,128]{3,1,0,2:T(8,128)(2,1)} %copy.569) | copy-start | bytes 1327108
  99.8 4.3 %copy-start.4 = (bf16[30,128,256]{2,1,0:T(8,128)(2,1)S(1)}, bf16[30,128,256]{2,1,0:T(8,128)(2,1)}, u32[]{:S(2)}) copy-start(bf16[30,128,256]{2,1,0:T(8,128)(2,1)} %copy-done.3) | copy-start | bytes 5898244
  103.1 1.3 copy-start.12
  106.5 0.6 copy-start.18
  123.2 4.5 %copy-start.20 = (bf16[4,192,96]{2,1,0:T(8,128)(2,1)S(1)}, bf16[4,192,96]{2,1,0:T(8,128)(2,1)}, u32[]{:S(2)}) copy-start(bf16[4,192,96]{2,1,0:T(8,128)(2,1)} %get-tuple-element.30) | copy-start | bytes 442372
Sparse Core Ops, SparseCore 0:
  10.2 29.1 all-gather.4
  41.0 28.6 all-gather.6

commit v2 on v1

--- a/solution.py
+++ b/solution.py
@@ -16,10 +16,10 @@
 VMEM = pl.BlockSpec(memory_space=pltpu.VMEM)
 RIM = 16
 UP_RIM = 4
-UNROLL = 2
-
-
-def start_kernel(rows_of, cols_of, pix_ref, up_ref, pix_out, up_out, sends, pix_recv, rim_recv, up_recv, own_sems):
+UNROLL = 4
+
+
+def start_kernel(rows_of, cols_of, pix_ref, up_ref, pix_out, up_out, sends, pix_recv, rim_recv, up_recv):
     row, col = lax.axis_index("row"), lax.axis_index("col")
     tall, up_rows = pix_ref.shape[0], up_ref.shape[0]
     barrier = pltpu.get_barrier_semaphore()
@@ -88,10 +88,8 @@
 
     for k in range(1, cols_of):
         tile_copy(k).start()
-    own_pix = pltpu.make_async_copy(pix_ref, pix_out.at[0, RIM : RIM + tall], own_sems.at[0])
-    own_up = pltpu.make_async_copy(up_ref, up_out.at[UP_RIM : UP_RIM + up_rows], own_sems.at[1])
-    own_pix.start()
-    own_up.start()
+    pix_out[0, RIM : RIM + tall] = pix_ref[...]
+    up_out[UP_RIM : UP_RIM + up_rows] = up_ref[...]
 
     @pl.when(row == 0)
     def _():
@@ -105,8 +103,6 @@
             pix_out[k, RIM + tall : tall + 2 * RIM] = jnp.zeros((RIM, pix_ref.shape[1]), BF)
         up_out[UP_RIM + up_rows : up_rows + 2 * UP_RIM] = jnp.zeros((UP_RIM,) + up_ref.shape[1:], BF)
 
-    own_pix.wait()
-    own_up.wait()
     for k in range(1, cols_of):
         tile_copy(k).wait()
     for side, there in sides:
@@ -140,7 +136,6 @@
             pltpu.SemaphoreType.DMA((4, cols_of)),
             pltpu.SemaphoreType.DMA((cols_of,)),
             pltpu.SemaphoreType.DMA((2, cols_of)),
-            pltpu.SemaphoreType.DMA((2,)),
             pltpu.SemaphoreType.DMA((2,)),
         ],
         compiler_params=pltpu.CompilerParams(collective_id=0, has_side_effects=True),
@@ -275,7 +270,7 @@
         in_specs=[VMEM] * len(ops),
         out_specs=VMEM if backward else (VMEM, VMEM),
         scratch_shapes=[pltpu.VMEM((tall, cols, 3 * chans), BF)],
-        compiler_params=pltpu.CompilerParams(vmem_limit_bytes=48 * 1024 * 1024),
+        compiler_params=pltpu.CompilerParams(vmem_limit_bytes=24 * 1024 * 1024),
         cost_estimate=pl.CostEstimate(
             flops=18 * rows * cols * chans * outs, bytes_accessed=4 * rows * cols * outs, transcendentals=0
         ),
@@ -306,7 +301,7 @@
         in_specs=[VMEM] * 2,
         out_specs=VMEM,
         scratch_shapes=[pltpu.VMEM((rows + 2, field.shape[1], 3 * chans), BF)],
-        compiler_params=pltpu.CompilerParams(vmem_limit_bytes=48 * 1024 * 1024),
+        compiler_params=pltpu.CompilerParams(vmem_limit_bytes=24 * 1024 * 1024),
         cost_estimate=pl.CostEstimate(
             flops=18 * rows * field.shape[1] * chans * delta.shape[2], bytes_accessed=4 * delta.size, transcendentals=0
         ),

time: 138 us -> 134 us (0.971)
  Pallas kernels: 79.2 us -> 69.7 us
  local copies, waits for them, and re-layouts: 29.2 us -> 32.6 us
  waiting for transfers between devices: 4.99 us -> 6.89 us
    pallas_call x7, Pallas kernels: 41.5 us -> 32 us  [conv_call(): pl.pallas_call(functools.partial(conv_kernel, halo, span, pre_from, backw...]
    unnamed x64 -> x70, local copies, waits for them, and re-layouts: 14.6 us -> 17.8 us
    all_gather x2, waiting for transfers between devices: 4.96 us -> 6.85 us  [col_gather(): return lax.all_gather(block, 'col', axis=0)]
  transfers between devices with their start and end apart: 2 -> 2, of which waited for: 1 -> 1; matrix products, arithmetic and copies ran while one was open for 13% -> 13% of each run, Pallas kernels for 23% -> 21%
where the time goes in v2:
time: 134 us; the launch traced here: 133 us
  Pallas kernels  69.7 us (52%)
  local copies, waits for them, and re-layouts  32.6 us (24%)
  between operations  14.6 us (11%)
  waiting for transfers between devices  6.89 us (5%)
  other arithmetic  6.78 us (5%)
  matrix products  2.64 us (2%)
    pallas_call x7, Pallas kernels, conv_call(): pl.pallas_call(functools.partial(conv_kernel, halo, span, pre_from, backw...  32 us
    unnamed x70, local copies, waits for them, and re-layouts  17.8 us
    pallas_call x1, Pallas kernels, row_sum_kernel(): pl.pallas_call(functools.partial(sum_kernel, rows_of, count), out_shape=t...  16 us
    pallas_call x1, Pallas kernels, start(): pl.pallas_call(functools.partial(start_kernel, rows_of, cols_of), out_sha...  12.6 us
    pallas_call x4, Pallas kernels, kernel_grad(): pl.pallas_call(functools.partial(grad_kernel, scale, field_from, delta_fr...  9.07 us
    all_gather x2, waiting for transfers between devices, col_gather(): return lax.all_gather(block, 'col', axis=0)  6.85 us
  transfers between devices with their start and end apart: 2, of which 1 were waited for; matrix products, arithmetic and copies ran while one was open for 13% of the time, Pallas kernels for 21%

profile of v2, /device:TPU:0, one launch (start us, length us, event | category | flops | bytes accessed | tf_op | source)
XLA Modules:
  0.0 133.3 jit_solution(6426407718842146688)
XLA Ops:
  7.2 1.7 %pad_maximum_fusion = bf16[3,3,32,320]{3,2,1,0:T(8,128)(2,1)} fusion(bf16[3,3,32,64]{3,2,1,0:T(8,128)(2,1)} %bitcast.187, bf16[3,3,32,256]{3,2,1,0:T(8,128)(2,1)} %bitcast.182), kind=kLoop, calls=%fused_computation.13 | loop fusion | flops 368640 | bytes 368640 | tf_op jit(solution)/shard_map/concatenate | solution.py:357
  10.5 1.6 %copy.632 = bf16[32,24,128]{2,0,1:T(8,128)(2,1)} copy(bf16[32,24,128]{2,1,0:T(8,128)(2,1)} %param.13) | data formatting | bytes 393216 | tf_op args[6]
  12.1 12.6 %shard_map.110 = (bf16[8,80,96]{2,1,0:T(8,128)(2,1)}, bf16[32,32,128]{2,1,0:T(8,128)(2,1)}) custom-call(bf16[48,96]{1,0:T(8,128)(2,1)} %copy.556.pix_ref, bf16[24,32,128]{2,1,0:T(8,128)(2,1)} %bitcast.176), custom_call_target="tpu_custom_call" | custom-call | tf_op jit(solution)/shard_map/pallas_call | solution.py:127
  24.7 2.3 %copy.557 = bf16[32,32,128]{1,2,0:T(8,128)(2,1)} copy(bf16[32,32,128]{2,1,0:T(8,128)(2,1)} %get-tuple-element.18) | data formatting | bytes 524288 | tf_op jit(solution)/shard_map/pallas_call | solution.py:127
  32.8 2.4 %select_convert_fusion = (bf16[36,128,64]{2,1,0:T(8,128)(2,1)S(1)}, f32[36,128,64]{2,1,0:T(8,128)}) fusion(pred[36]{0:T(512)(128)(4,1)S(1)} %compare_and_fusion.1, bf16[64,48,1]{0,1,2:T(8,128)(2,1)S(1)} %bitcast.156, bf16[6,8,36,128]{3,2,1,0:T(8,128)(2,1)S(1)} %bitcast.178), kind=kOutput, calls=%fused_computation.1 | convolution fusion | flops 30081024 | bytes 2218020 | tf_op jit(solution)/shard_map/dot_general | solution.py:373
  35.2 4.1 %shard_map.111 = (f32[34,128,64]{2,1,0:T(8,128)S(1)}, bf16[34,128,64]{2,1,0:T(8,128)(2,1)S(1)}) custom-call(bf16[36,128,64]{2,1,0:T(8,128)(2,1)S(1)} %get-tuple-element.64.field_ref, bf16[3,192,64]{2,1,0:T(8,128)(2,1)S(1)} %bitcast.167), custom_call_target="tpu_custom_call" | custom-call | flops 320864256 | bytes 1114112 | tf_op jit(solution)/shard_map/pallas_call | solution.py:267
  39.3 1.4 %copy-done.7 = f32[34,128,64]{2,1,0:T(8,128)} copy-done((f32[34,128,64]{2,1,0:T(8,128)}, f32[34,128,64]{2,1,0:T(8,128)S(1)}, u32[]{:S(2)}) %copy-start.7) | copy-done | bytes 1114136
  40.7 3.8 %shard_map.112 = (f32[32,128,64]{2,1,0:T(8,128)S(1)}, bf16[32,128,64]{2,1,0:T(8,128)(2,1)S(1)}) custom-call(bf16[34,128,64]{2,1,0:T(8,128)(2,1)S(1)} %get-tuple-element.20.field_ref, bf16[3,192,64]{2,1,0:T(8,128)(2,1)S(1)} %bitcast.166), custom_call_target="tpu_custom_call" | custom-call | flops 301989888 | bytes 1048576 | tf_op jit(solution)/shard_map/pallas_call | solution.py:267
  45.5 1.4 %copy-done.9 = f32[32,128,64]{2,1,0:T(8,128)} copy-done((f32[32,128,64]{2,1,0:T(8,128)}, f32[32,128,64]{2,1,0:T(8,128)S(1)}, u32[]{:S(2)}) %copy-start.9) | copy-done | bytes 1048600
  47.9 1.9 %copy.566 = bf16[8,3,3,32,320]{4,3,0,2,1:T(8,128)(2,1)S(1)} copy(bf16[8,3,3,32,320]{4,3,2,1,0:T(8,128)(2,1)} %bitcast.175) | data formatting | bytes 2949120 | tf_op jit(solution)/shard_map/all_gather | solution.py:312
  53.4 4.2 %shard_map.113 = (f32[30,128,256]{2,1,0:T(8,128)S(1)}, bf16[30,128,256]{2,1,0:T(8,128)(2,1)S(1)}) custom-call(bf16[32,128,64]{2,1,0:T(8,128)(2,1)S(1)} %copy-done.12, bf16[3,192,256]{2,1,0:T(8,128)(2,1)S(1)} %bitcast.170), custom_call_target="tpu_custom_call" | custom-call | flops 1132462080 | bytes 3932160 | tf_op jit(solution)/shard_map/pallas_call | solution.py:267
  57.5 1.9 %copy-done.21 = f32[30,128,256]{2,1,0:T(8,128)} copy-done((f32[30,128,256]{2,1,0:T(8,128)}, f32[30,128,256]{2,1,0:T(8,128)S(1)}, u32[]{:S(2)}) %copy-start.21) | copy-done | bytes 3932184
  59.4 2.8 %shard_map.114 = bf16[3,256,96]{2,1,0:T(8,128)(2,1)S(1)} custom-call(bf16[32,128,32]{2,1,0:T(8,128)(2,1)S(1)} %bitcast.160, bf16[30,128,256]{2,1,0:T(8,128)(2,1)S(1)} %get-tuple-element.22.delta_ref), custom_call_target="tpu_custom_call" | custom-call | flops 452984832 | bytes 3932160 | tf_op jit(solution)/shard_map/pallas_call | solution.py:298
  62.9 6.9 %all-gather.7.cloned.1.call-done = bf16[256,32,128]{2,1,0:T(8,128)(2,1)} async-done(((bf16[32,32,128]{2,1,0:T(8,128)(2,1)}), bf16[256,32,128]{2,1,0:T(8,128)(2,1)}) %all-gather.7.cloned.1.call-update) | async-done | bytes 2097168 | tf_op jit(solution)/shard_map/all_gather | solution.py:312
  69.7 1.6 %copy-done.20 = bf16[256,32,128]{2,1,0:T(8,128)(2,1)S(1)} copy-done((bf16[256,32,128]{2,1,0:T(8,128)(2,1)S(1)}, bf16[256,32,128]{2,1,0:T(8,128)(2,1)}, u32[]{:S(2)}) %copy-start.20) | copy-done | bytes 2097176
  71.3 2.1 %copy-done.22 = f32[30,128,256]{2,1,0:T(8,128)S(1)} copy-done((f32[30,128,256]{2,1,0:T(8,128)S(1)}, f32[30,128,256]{2,1,0:T(8,128)}, u32[]{:S(2)}) %copy-start.22) | copy-done | bytes 3932184
  73.4 8.0 %shard_map.115.field_ref = bf16[30,128,256]{2,1,0:T(8,128)(2,1)S(1)} custom-call(bf16[8,32,32,128]{3,2,1,0:T(8,128)(2,1)S(1)} %bitcast.172, bf16[3,768,320]{2,1,0:T(8,128)(2,1)S(1)} %bitcast.158, f32[30,128,256]{2,1,0:T(8,128)S(1)} %copy-done.22), custom_call_target="tpu_custom_call" | custom-call | flops 4529848320 | bytes 3932160 | tf_op jit(solution)/shard_map/pallas_call | solution.py:267
  81.4 6.0 %shard_map.116.field_ref.delta_ref = bf16[28,128,64]{2,1,0:T(8,128)(2,1)S(1)} custom-call(bf16[30,128,256]{2,1,0:T(8,128)(2,1)S(1)} %shard_map.115.field_ref, bf16[3,768,320]{2,1,0:T(8,128)(2,1)S(1)} %bitcast.159, f32[32,128,64]{2,1,0:T(8,128)S(1)} %copy-done.10), custom_call_target="tpu_custom_call" | custom-call | flops 1056964608 | bytes 917504 | tf_op jit(solution)/shard_map/pallas_call | solution.py:267
  87.5 2.1 %shard_map.120 = bf16[3,64,192]{2,1,0:T(8,128)(2,1)S(1)} custom-call(bf16[34,128,64]{2,1,0:T(8,128)(2,1)S(1)} %copy-done.2, bf16[28,128,64]{2,1,0:T(8,128)(2,1)S(1)} %shard_map.116.field_ref.delta_ref), custom_call_target="tpu_custom_call" | custom-call | flops 226492416 | bytes 917504 | tf_op jit(solution)/shard_map/pallas_call | solution.py:298
  90.2 3.2 %shard_map.117.field_ref.delta_ref = bf16[26,128,64]{2,1,0:T(8,128)(2,1)S(1)} custom-call(bf16[28,128,64]{2,1,0:T(8,128)(2,1)S(1)} %shard_map.116.field_ref.delta_ref, bf16[3,192,64]{2,1,0:T(8,128)(2,1)S(1)} %bitcast.163, f32[34,128,64]{2,1,0:T(8,128)S(1)} %copy-done.8), custom_call_target="tpu_custom_call" | custom-call | flops 245366784 | bytes 851968 | tf_op jit(solution)/shard_map/pallas_call | solution.py:267
  93.4 2.1 %shard_map.119 = bf16[3,64,192]{2,1,0:T(8,128)(2,1)S(1)} custom-call(bf16[36,128,64]{2,1,0:T(8,128)(2,1)S(1)} %get-tuple-element.64.field_ref, bf16[26,128,64]{2,1,0:T(8,128)(2,1)S(1)} %shard_map.117.field_ref.delta_ref), custom_call_target="tpu_custom_call" | custom-call | flops 226492416 | bytes 851968 | tf_op jit(solution)/shard_map/pallas_call | solution.py:298
  96.1 2.8 %shard_map.118 = bf16[24,128,64]{2,1,0:T(8,128)(2,1)S(1)} custom-call(bf16[26,128,64]{2,1,0:T(8,128)(2,1)S(1)} %shard_map.117.field_ref.delta_ref, bf16[3,192,64]{2,1,0:T(8,128)(2,1)S(1)} %bitcast.165, f32[36,128,64]{2,1,0:T(8,128)S(1)} %copy-done.6), custom_call_target="tpu_custom_call" | custom-call | flops 226492416 | bytes 786432 | tf_op jit(solution)/shard_map/pallas_call | solution.py:267
  100.3 2.1 %shard_map.121 = bf16[3,32,192]{2,1,0:T(8,128)(2,1)S(1)} custom-call(bf16[32,128,64]{2,1,0:T(8,128)(2,1)S(1)} %copy-done.13, bf16[30,128,32]{2,1,0:T(8,128)(2,1)S(1)} %constant_dynamic-slice_fusion.delta_ref), custom_call_target="tpu_custom_call" | custom-call | flops 113246208 | bytes 491520 | tf_op jit(solution)/shard_map/pallas_call | solution.py:298
  103.0 16.0 %shard_map.122 = (bf16[4,192,96]{2,1,0:T(8,128)(2,1)}, bf16[4,16,48]{2,1,0:T(8,128)(2,1)}, bf16[4,48,192]{2,1,0:T(8,128)(2,1)}, bf16[4,48,192]{2,1,0:T(8,128)(2,1)}, bf16[4,24,192]{2,1,0:T(8,128)(2,1)}) custom-call(bf16[4,192,96]{2,1,0:T(8,128)(2,1)} %bitcast.161, bf16[4,16,48]{2,1,0:T(8,128)(2,1)} %bitcast.188, bf16[4,48,192]{2,1,0:T(8,128)(2,1)} %bitcast.169, ...), custom_call_target="tpu_custom_call" | custom-call | tf_op jit(solution)/shard_map/pallas_call | solution.py:189
  (106 shorter events, 23.9 us)
Async XLA Ops:
  7.2 25.6 %copy-start = (bf16[64,3,4,4]{0,3,2,1:T(4,128)(2,1)S(1)}, bf16[64,3,4,4]{0,3,2,1:T(4,128)(2,1)}, u32[]{:S(2)}) copy-start(bf16[64,3,4,4]{0,3,2,1:T(4,128)(2,1)} %param.8) | copy-start | bytes 18436
  7.2 40.7 %all-gather.5.cloned.1.call-start = ((), (), s32[]{:S(2)}) async-start(), calls=%async_computation | async-start | bytes 1990656 | tf_op jit(solution)/shard_map/all_gather | solution.py:312
  8.9 60.8 %all-gather.7.cloned.1.call-start = ((), (), s32[]{:S(2)}) async-start(), calls=%async_computation.1 | async-start | bytes 2359296 | tf_op jit(solution)/shard_map/all_gather | solution.py:312
  30.4 2.1 %copy-start.16 = (bf16[64,64,3,3]{1,0,3,2:T(8,128)(2,1)S(1)}, bf16[64,64,3,3]{1,0,3,2:T(8,128)(2,1)}, u32[]{:S(2)}) copy-start(bf16[64,64,3,3]{1,0,3,2:T(8,128)(2,1)} %param.9) | copy-start | bytes 221188
  30.6 2.0 %copy-start.15 = (bf16[64,64,3,3]{1,0,3,2:T(8,128)(2,1)S(1)}, bf16[64,64,3,3]{1,0,3,2:T(8,128)(2,1)}, u32[]{:S(2)}) copy-start(bf16[64,64,3,3]{1,0,3,2:T(8,128)(2,1)} %param.10) | copy-start | bytes 221188
  39.3 1.4 %copy-start.7 = (f32[34,128,64]{2,1,0:T(8,128)}, f32[34,128,64]{2,1,0:T(8,128)S(1)}, u32[]{:S(2)}) copy-start(f32[34,128,64]{2,1,0:T(8,128)S(1)} %get-tuple-element.25.refs_0_) | copy-start | bytes 3342340
  44.5 1.0 copy-start.1
  45.5 1.4 %copy-start.9 = (f32[32,128,64]{2,1,0:T(8,128)}, f32[32,128,64]{2,1,0:T(8,128)S(1)}, u32[]{:S(2)}) copy-start(f32[32,128,64]{2,1,0:T(8,128)S(1)} %get-tuple-element.24.refs_0_) | copy-start | bytes 3145732
  46.9 1.0 copy-start.11
  52.0 7.4 %copy-start.5 = (bf16[32,32,128]{1,2,0:T(8,128)(2,1)S(1)}, bf16[32,32,128]{1,2,0:T(8,128)(2,1)}, u32[]{:S(2)}) copy-start(bf16[32,32,128]{1,2,0:T(8,128)(2,1)} %copy.557) | copy-start | bytes 786436
  52.0 1.3 %copy-start.12 = (bf16[32,128,64]{2,1,0:T(8,128)(2,1)S(1)}, bf16[32,128,64]{2,1,0:T(8,128)(2,1)}, u32[]{:S(2)}) copy-start(bf16[32,128,64]{2,1,0:T(8,128)(2,1)} %copy-done.11) | copy-start | bytes 1572868
  57.5 1.9 %copy-start.21 = (f32[30,128,256]{2,1,0:T(8,128)}, f32[30,128,256]{2,1,0:T(8,128)S(1)}, u32[]{:S(2)}) copy-start(f32[30,128,256]{2,1,0:T(8,128)S(1)} %get-tuple-element.23.refs_0_) | copy-start | bytes 11796484
  62.2 0.7 copy-start.14
  69.7 1.6 %copy-start.20 = (bf16[256,32,128]{2,1,0:T(8,128)(2,1)S(1)}, bf16[256,32,128]{2,1,0:T(8,128)(2,1)}, u32[]{:S(2)}) copy-start(bf16[256,32,128]{2,1,0:T(8,128)(2,1)} %all-gather.7.cloned.1.call-done) | copy-start | bytes 6291460
  71.3 2.1 %copy-start.22 = (f32[30,128,256]{2,1,0:T(8,128)S(1)}, f32[30,128,256]{2,1,0:T(8,128)}, u32[]{:S(2)}) copy-start(f32[30,128,256]{2,1,0:T(8,128)} %copy-done.21) | copy-start | bytes 11796484
  73.4 8.0 %copy-start.10 = (f32[32,128,64]{2,1,0:T(8,128)S(1)}, f32[32,128,64]{2,1,0:T(8,128)}, u32[]{:S(2)}) copy-start(f32[32,128,64]{2,1,0:T(8,128)} %copy-done.9) | copy-start | bytes 3145732
  81.4 6.0 %copy-start.3 = (bf16[30,128,256]{2,1,0:T(8,128)(2,1)}, bf16[30,128,256]{2,1,0:T(8,128)(2,1)S(1)}, u32[]{:S(2)}) copy-start(bf16[30,128,256]{2,1,0:T(8,128)(2,1)S(1)} %shard_map.115.field_ref) | copy-start | bytes 5898244
  81.4 6.0 %copy-start.2 = (bf16[34,128,64]{2,1,0:T(8,128)(2,1)S(1)}, bf16[34,128,64]{2,1,0:T(8,128)(2,1)}, u32[]{:S(2)}) copy-start(bf16[34,128,64]{2,1,0:T(8,128)(2,1)} %copy-done.1) | copy-start | bytes 1671172
  81.4 8.8 %copy-start.8 = (f32[34,128,64]{2,1,0:T(8,128)S(1)}, f32[34,128,64]{2,1,0:T(8,128)}, u32[]{:S(2)}) copy-start(f32[34,128,64]{2,1,0:T(8,128)} %copy-done.7) | copy-start | bytes 3342340
  90.2 5.9 %copy-start.6 = (f32[36,128,64]{2,1,0:T(8,128)S(1)}, f32[36,128,64]{2,1,0:T(8,128)}, u32[]{:S(2)}) copy-start(f32[36,128,64]{2,1,0:T(8,128)} %get-tuple-element.65.refs_0_) | copy-start | bytes 3538948
  96.1 2.8 %copy-start.24 = (bf16[3,16,36,128]{3,1,0,2:T(8,128)(2,1)S(1)}, bf16[3,16,36,128]{3,1,0,2:T(8,128)(2,1)}, u32[]{:S(2)}) copy-start(bf16[3,16,36,128]{3,1,0,2:T(8,128)(2,1)} %copy.569) | copy-start | bytes 1327108
  96.1 3.8 %copy-start.4 = (bf16[30,128,256]{2,1,0:T(8,128)(2,1)S(1)}, bf16[30,128,256]{2,1,0:T(8,128)(2,1)}, u32[]{:S(2)}) copy-start(bf16[30,128,256]{2,1,0:T(8,128)(2,1)} %copy-done.3) | copy-start | bytes 5898244
  99.0 1.3 %copy-start.13 = (bf16[32,128,64]{2,1,0:T(8,128)(2,1)S(1)}, bf16[32,128,64]{2,1,0:T(8,128)(2,1)}, u32[]{:S(2)}) copy-start(bf16[32,128,64]{2,1,0:T(8,128)(2,1)} %copy-done.11) | copy-start | bytes 1572868
  119.0 4.5 %copy-start.23 = (bf16[4,192,96]{2,1,0:T(8,128)(2,1)S(1)}, bf16[4,192,96]{2,1,0:T(8,128)(2,1)}, u32[]{:S(2)}) copy-start(bf16[4,192,96]{2,1,0:T(8,128)(2,1)} %get-tuple-element.30) | copy-start | bytes 442372
  (3 other events, 1.9 us)
Sparse Core Ops, SparseCore 0:
  10.2 29.1 all-gather.4
  41.0 28.6 all-gather.6
